TPU v7x, 32 devices: a whole 2x2x4 slice. The times are simulated.
32 devices in a mesh: pair: 8 (over z, x), rows: 4 (over y, core).
Axes of the slice: x: 2, y: 2, z: 4, core: 2. Of those that a mesh axis runs over, the one named last changes fastest.
Arguments:
- matrix: float32 [16384, 2048], P('rows', 'pair')
- plan: int32 [3, 8], P(None, 'pair'), may hold values 0 or 1
Outputs:
- rotated: float32 [16384, 2048], P('rows', 'pair')
- offness: float32 [3], replicated
All inputs are finite; a program needn't handle non-finite values. No bound on the sum of `plan` on one device may be relied on, other than what follows from the above.
Results may differ from a plain program's by a relative error of at most 0.00025.
Values sent between devices are 32-bit elements; how exact they have to be, the bound alone decides.
A program may use at most 64 MiB of HBM per device.

v0:
```python
import jax
import jax.numpy as jnp
from jax import lax
from jax.sharding import PartitionSpec as P

ROUNDS = 3


def from_behind(x, axis, by):
    peers = lax.axis_size(axis)
    return lax.ppermute(x, axis, [(i, (i + by) % peers) for i in range(peers)])


def off_total(value):
    return lax.psum(value, "pair")


def pass_on(block):
    return from_behind(block, "pair", 1)


def make_rotation(gram, mean_sq, eye, weights):
    diagonal = jnp.diagonal(gram)
    denom = diagonal[:, None] + diagonal[None, :] + mean_sq
    skew = gram * (weights[None, :] - weights[:, None]) / denom
    square = jnp.dot(skew, skew, precision=lax.Precision.HIGHEST)
    plus = eye + skew
    numer = jnp.dot(plus, plus, precision=lax.Precision.HIGHEST)
    lower = jnp.linalg.cholesky(eye - square)
    return jax.scipy.linalg.cho_solve((lower, True), numer)


def local(matrix, plan):
    width = matrix.shape[1]
    half = width // 2
    pair_count = lax.axis_size("pair")
    ncols_all = width * pair_count
    eye = jnp.eye(width, dtype=jnp.float32)
    weights = jnp.arange(width, dtype=jnp.float32) / jnp.float32(width - 1)
    mean_sq = lax.psum(jnp.sum(matrix * matrix), ("pair", "rows")) / ncols_all
    current = matrix
    values = []
    for step in range(ROUNDS):
        partial_gram = lax.dot_general(
            current,
            current,
            (((0,), (0,)), ((), ())),
            precision=lax.Precision.HIGHEST,
            preferred_element_type=jnp.float32,
        )
        gram = lax.psum(partial_gram, "rows")
        offdiag = gram * (1.0 - eye)
        off_local = jnp.sum(offdiag * offdiag)
        if step == 0:
            total_off = off_total(off_local)
        else:
            total_off = off_total(off_local)
        values.append(jnp.sqrt(total_off / (pair_count * width * (width - 1))) / mean_sq)
        rotation = make_rotation(gram, mean_sq, eye, weights)
        keep_last = plan[step, 0] == 1
        turned = jnp.dot(current, rotation, precision=lax.Precision.HIGHEST)
        first_half = turned[:, :half]
        second_half = turned[:, half:]
        kept = jnp.where(keep_last, second_half, first_half)
        moving = jnp.where(keep_last, first_half, second_half)
        arrived = pass_on(moving)
        current = jnp.concatenate([kept, arrived], axis=1)
    return (current, jnp.stack(values))


def solution(mesh):
    in_specs = (P("rows", "pair"), P(None, "pair"))
    out_specs = (P("rows", "pair"), P())
    return jax.shard_map(local, mesh=mesh, in_specs=in_specs, out_specs=out_specs, check_vma=False)
```

profile of v0, /device:TPU:0, one launch (start us, length us, event | category | flops | bytes accessed | tf_op | source)
XLA Modules:
  0.0 539.2 jit_solution(11518162019927558470)
XLA Ops:
  7.2 10.9 %fusion.76 = f32[256,256]{0,1:T(8,128)} fusion(f32[4096,256]{1,0:T(8,128)} %param.5), kind=kOutput, calls=%fused_computation.150 | convolution fusion | flops 3221225472 | bytes 4456448 | tf_op jit(solution)/shard_map/dot_general | solution.py:44
  22.7 42.5 %psum.50 = f32[]{:T(128)} all-reduce(f32[]{:T(128)} %multiply_reduce_fusion), channel_id=1, replica_groups=mesh['pair'=8,'rows'=4] {'pair','rows'}, use_global_device_ids=true, to_apply=%region_2.0 | all-reduce | flops 1 | bytes 8 | tf_op jit(solution)/shard_map/psum | solution.py:40
  71.0 11.7 %cholesky.172 = f32[128,128]{1,0:T(8,128)S(1)} custom-call(f32[128,128]{1,0:T(8,128)S(1)} %cholesky.270), custom_call_target="Cholesky" | custom-call | tf_op jit(solution)/shard_map/jit(cholesky)/cholesky | solution.py:29
  82.8 9.8 %custom-call.23 = f32[1,128,128]{1,2,0:T(8,128)S(1)} custom-call(f32[1,128,128]{2,1,0:T(8,128)S(1)} %get-tuple-element.81), custom_call_target="InvertDiagBlocksLowerTriangular" | custom-call | tf_op jit(solution)/shard_map/jit(cholesky)/cholesky | solution.py:29
  93.1 11.7 %cholesky.189 = f32[128,128]{1,0:T(8,128)S(1)} custom-call(f32[128,128]{1,0:T(8,128)S(1)} %convolution_subtract_fusion.11), custom_call_target="Cholesky" | custom-call | tf_op jit(solution)/shard_map/jit(cholesky)/cholesky | solution.py:29
  110.9 19.8 %custom-call.24 = f32[2,128,128]{1,2,0:T(8,128)S(1)} custom-call(f32[2,128,128]{2,1,0:T(8,128)S(1)} %get-tuple-element.24), custom_call_target="InvertDiagBlocksLowerTriangular" | custom-call | tf_op jit(solution)/shard_map/jit(_cho_solve)/triangular_solve | solution.py:30
  133.3 8.8 %convolution_bitcast_fusion = f32[4096,256]{0,1:T(8,128)S(1)} fusion(f32[4096,256]{1,0:T(8,128)} %param.5, f32[128,256]{1,0:T(8,128)S(1)} %fusion.47, f32[128,256]{1,0:T(8,128)S(1)} %fusion.46), kind=kOutput, calls=%fused_computation.9 | convolution fusion | flops 3221291008 | bytes 8650752 | tf_op jit(solution)/shard_map/dot_general | solution.py:61
  144.8 47.0 %collective-permute-done = f32[4096,128]{0,1:T(8,128)S(1)} collective-permute-done((f32[4096,128]{0,1:T(8,128)S(1)}, f32[4096,128]{0,1:T(8,128)S(1)}, u32[]{:S(2)}, u32[]{:S(2)}) %collective-permute-start) | collective-permute-done | bytes 2097184 | tf_op jit(solution)/shard_map/ppermute | solution.py:11
  193.1 4.2 fusion.3
  198.2 28.8 %all-reduce.8.cloned.1.call-done = f32[256,256]{0,1:T(8,128)} async-done(((f32[256,256]{0,1:T(8,128)}), f32[256,256]{0,1:T(8,128)}) %all-reduce.8.cloned.1.call-update) | async-done | bytes 262160 | tf_op jit(solution)/shard_map/psum | solution.py:51
  231.4 11.7 %cholesky.206 = f32[128,128]{1,0:T(8,128)S(1)} custom-call(f32[128,128]{1,0:T(8,128)S(1)} %cholesky.273), custom_call_target="Cholesky" | custom-call | tf_op jit(solution)/shard_map/jit(cholesky)/cholesky | solution.py:29
  243.9 9.8 %custom-call.25 = f32[1,128,128]{1,2,0:T(8,128)S(1)} custom-call(f32[1,128,128]{2,1,0:T(8,128)S(1)} %get-tuple-element.77), custom_call_target="InvertDiagBlocksLowerTriangular" | custom-call | tf_op jit(solution)/shard_map/jit(cholesky)/cholesky | solution.py:29
  254.2 11.7 %cholesky.223 = f32[128,128]{1,0:T(8,128)S(1)} custom-call(f32[128,128]{1,0:T(8,128)S(1)} %convolution_subtract_fusion.10), custom_call_target="Cholesky" | custom-call | tf_op jit(solution)/shard_map/jit(cholesky)/cholesky | solution.py:29
  268.0 4.5 while.7
  272.5 19.7 %custom-call.26 = f32[2,128,128]{1,2,0:T(8,128)S(1)} custom-call(f32[2,128,128]{2,1,0:T(8,128)S(1)} %get-tuple-element.25), custom_call_target="InvertDiagBlocksLowerTriangular" | custom-call | tf_op jit(solution)/shard_map/jit(_cho_solve)/triangular_solve | solution.py:30
  300.7 47.2 %collective-permute-done.1 = f32[4096,128]{0,1:T(8,128)S(1)} collective-permute-done((f32[4096,128]{0,1:T(8,128)S(1)}, f32[4096,128]{0,1:T(8,128)S(1)}, u32[]{:S(2)}, u32[]{:S(2)}) %collective-permute-start.1) | collective-permute-done | bytes 2097184 | tf_op jit(solution)/shard_map/ppermute | solution.py:11
  349.3 4.2 fusion.1
  354.1 29.9 %all-reduce.10.cloned.1.call-done = f32[256,256]{0,1:T(8,128)} async-done(((f32[256,256]{0,1:T(8,128)}), f32[256,256]{0,1:T(8,128)}) %all-reduce.10.cloned.1.call-update) | async-done | bytes 262160 | tf_op jit(solution)/shard_map/psum | solution.py:51
  389.1 11.7 %cholesky.240 = f32[128,128]{1,0:T(8,128)S(1)} custom-call(f32[128,128]{1,0:T(8,128)S(1)} %cholesky.276), custom_call_target="Cholesky" | custom-call | tf_op jit(solution)/shard_map/jit(cholesky)/cholesky | solution.py:29
  401.5 9.8 %custom-call.27 = f32[1,128,128]{1,2,0:T(8,128)S(1)} custom-call(f32[1,128,128]{2,1,0:T(8,128)S(1)} %get-tuple-element.73), custom_call_target="InvertDiagBlocksLowerTriangular" | custom-call | tf_op jit(solution)/shard_map/jit(cholesky)/cholesky | solution.py:29
  413.5 11.9 %cholesky.257 = f32[128,128]{1,0:T(8,128)S(1)} custom-call(f32[128,128]{1,0:T(8,128)S(1)} %convolution_subtract_fusion.9), custom_call_target="Cholesky" | custom-call | tf_op jit(solution)/shard_map/jit(cholesky)/cholesky | solution.py:29
  431.2 19.7 %custom-call.28 = f32[2,128,128]{1,2,0:T(8,128)S(1)} custom-call(f32[2,128,128]{2,1,0:T(8,128)S(1)} %get-tuple-element.26), custom_call_target="InvertDiagBlocksLowerTriangular" | custom-call | tf_op jit(solution)/shard_map/jit(_cho_solve)/triangular_solve | solution.py:30
  462.7 57.4 %all-reduce.1 = (f32[]{:T(128)}, f32[]{:T(128)}, f32[]{:T(128)}) all-reduce(f32[]{:T(128)} %fusion.12, f32[]{:T(128)} %fusion.10, f32[]{:T(128)} %fusion.8), channel_id=1, replica_groups=mesh['pair'=8,'rows'=4] {'pair'}, use_global_device_ids=true, to_apply=%region_14.17 | all-reduce | flops 3 | bytes 24 | tf_op jit(solution)/shard_map/psum | solution.py:15
  526.8 5.6 %copy.23 = f32[4096,256]{1,0:T(8,128)} copy(f32[4096,256]{0,1:T(8,128)} %pad_maximum_fusion.2) | data formatting | bytes 8388608
  (127 shorter events, 77.8 us)
Async XLA Ops:
  7.2 59.4 %all-reduce.6.cloned.1.call-start = ((), (), s32[]{:S(2)}) async-start(), calls=%async_computation | async-start | bytes 524288 | tf_op jit(solution)/shard_map/psum | solution.py:51
  18.1 4.0 copy-start.8
  18.1 208.9 %all-reduce.8.cloned.1.call-start = ((), (), s32[]{:S(2)}) async-start(), calls=%async_computation.1 | async-start | bytes 524288 | tf_op jit(solution)/shard_map/psum | solution.py:51
  66.6 64.2 %copy-start = (f32[256,256]{0,1:T(8,128)S(1)}, f32[256,256]{0,1:T(8,128)}, u32[]{:S(2)}) copy-start(f32[256,256]{0,1:T(8,128)} %all-reduce.6.cloned.1.call-done) | copy-start | bytes 786436
  142.5 49.3 %collective-permute-start = (f32[4096,128]{0,1:T(8,128)S(1)}, f32[4096,128]{0,1:T(8,128)S(1)}, u32[]{:S(2)}, u32[]{:S(2)}) collective-permute-start(f32[4096,128]{0,1:T(8,128)S(1)} %get-tuple-element.69), channel_id=1, source_target_pairs={{0,4},{4,8},{8,12},{12,16},{16,20},{20,24},{24,28},{28,0},{1,5},{5... | collective-permute-start | bytes 6291464 | tf_op jit(solution)/shard_map/ppermute | solution.py:11
  191.8 1.3 copy-start.5
  197.3 186.7 %all-reduce.10.cloned.1.call-start = ((), (), s32[]{:S(2)}) async-start(), calls=%async_computation.2 | async-start | bytes 524288 | tf_op jit(solution)/shard_map/psum | solution.py:51
  227.0 65.1 %copy-start.1 = (f32[256,256]{0,1:T(8,128)S(1)}, f32[256,256]{0,1:T(8,128)}, u32[]{:S(2)}) copy-start(f32[256,256]{0,1:T(8,128)} %all-reduce.8.cloned.1.call-done) | copy-start | bytes 786436
  292.1 2.5 copy-start.6
  299.0 48.9 %collective-permute-start.1 = (f32[4096,128]{0,1:T(8,128)S(1)}, f32[4096,128]{0,1:T(8,128)S(1)}, u32[]{:S(2)}, u32[]{:S(2)}) collective-permute-start(f32[4096,128]{0,1:T(8,128)S(1)} %get-tuple-element.67), channel_id=1, source_target_pairs={{0,4},{4,8},{8,12},{12,16},{16,20},{20,24},{24,28},{28,0},{1,5},{5... | collective-permute-start | bytes 6291464 | tf_op jit(solution)/shard_map/ppermute | solution.py:11
  348.0 1.3 copy-start.3
  384.0 66.9 %copy-start.2 = (f32[256,256]{0,1:T(8,128)S(1)}, f32[256,256]{0,1:T(8,128)}, u32[]{:S(2)}) copy-start(f32[256,256]{0,1:T(8,128)} %all-reduce.10.cloned.1.call-done) | copy-start | bytes 786436
  388.4 0.7 copy-start.7
  450.9 2.5 copy-start.4
  459.2 63.7 %collective-permute-start.2 = (f32[4096,128]{0,1:T(8,128)}, f32[4096,128]{0,1:T(8,128)}, u32[]{:S(2)}, u32[]{:S(2)}) collective-permute-start(f32[4096,128]{0,1:T(8,128)} %get-tuple-element.65), channel_id=1, source_target_pairs={{0,4},{4,8},{8,12},{12,16},{16,20},{20,24},{24,28},{28,0},{1,5},{5... | collective-permute-start | bytes 6291464 | tf_op jit(solution)/shard_map/ppermute | solution.py:11
Sparse Core Ops, SparseCore 0:
  18.2 35.0 all-reduce.5
  197.5 29.4 all-reduce.7
  353.7 30.3 all-reduce.9
where the time goes:
time: 546 us; the launch traced here: 539 us
  other arithmetic  176 us (32%)
  waiting for transfers between devices  153 us (28%)
  blocking collectives  100 us (18%)
  matrix products  51.3 us (9%)
  local copies, waits for them, and re-layouts  29.9 us (5%)
  between operations  23 us (4%)
  starting transfers between devices  5.82 us (1%)
    another operation x20, other arithmetic, make_rotation(): lower = jnp.linalg.cholesky(eye - square)  103 us
    ppermute x3, waiting for transfers between devices, from_behind(): return lax.ppermute(x, axis, [(i, (i + by) % peers) for i in range(peers)])  94.2 us
    another operation x7, other arithmetic, make_rotation(): return jax.scipy.linalg.cho_solve((lower, True), numer)  59.3 us
    psum x3, waiting for transfers between devices, local(): gram = lax.psum(partial_gram, 'rows')  58.7 us
    psum x1, blocking collectives, off_total(): return lax.psum(value, 'pair')  57.4 us
    psum x1, blocking collectives, local(): mean_sq = lax.psum(jnp.sum(matrix * matrix), ('pair', 'rows')) / ncols_all  42.5 us
    dot_general x3, matrix products, local(): lax.dot_general(current, current, (((0,), (0,)), ((), ())), precision=lax...  19.4 us
    dot_general x3, matrix products, local(): turned = jnp.dot(current, rotation, precision=lax.Precision.HIGHEST)  16.8 us
  transfers between devices with their start and end apart: 6, of which 4 were waited for; matrix products, arithmetic and copies ran while one was open for 1% of the time, Pallas kernels for 0%

commit v1 on v0

--- a/solution.py
+++ b/solution.py
@@ -48,7 +48,9 @@
             precision=lax.Precision.HIGHEST,
             preferred_element_type=jnp.float32,
         )
-        gram = lax.psum(partial_gram, "rows")
+        gram = partial_gram
+        for hop in (1, 2):
+            gram = gram + lax.ppermute(gram, "rows", [(dev, dev ^ hop) for dev in range(4)])
         offdiag = gram * (1.0 - eye)
         off_local = jnp.sum(offdiag * offdiag)
         if step == 0:

time: 546 us -> 487 us (0.89)
  waiting for transfers between devices: 153 us -> 112 us
  between operations: 23 us -> 9.8 us
    psum x3 -> x0, waiting for transfers between devices: 58.7 us -> none  [local(): gram = lax.psum(partial_gram, 'rows')]
    ppermute x0 -> x6, waiting for transfers between devices: none -> 15.8 us  [local(): lax.ppermute(gram, 'rows', [(dev, dev ^ hop) for dev in range(4)])]
    ppermute x0 -> x6, starting transfers between devices: none -> 6.05 us  [local(): lax.ppermute(gram, 'rows', [(dev, dev ^ hop) for dev in range(4)])]
  transfers between devices with their start and end apart: 6 -> 9, of which waited for: 4 -> 6; matrix products, arithmetic and copies ran while one was open for 1% -> 1% of each run, Pallas kernels for 0% -> 0%
where the time goes in v1:
time: 487 us; the launch traced here: 482 us
  other arithmetic  173 us (36%)
  waiting for transfers between devices  112 us (23%)
  blocking collectives  102 us (21%)
  matrix products  48.2 us (10%)
  local copies, waits for them, and re-layouts  27.6 us (6%)
  between operations  9.8 us (2%)
  starting transfers between devices  8.44 us (2%)
    another operation x20, other arithmetic, make_rotation(): lower = jnp.linalg.cholesky(eye - square)  103 us
    ppermute x3, waiting for transfers between devices, from_behind(): return lax.ppermute(x, axis, [(i, (i + by) % peers) for i in range(peers)])  96.7 us
    psum x1, blocking collectives, off_total(): return lax.psum(value, 'pair')  59.8 us
    another operation x7, other arithmetic, make_rotation(): return jax.scipy.linalg.cho_solve((lower, True), numer)  59.3 us
    psum x1, blocking collectives, local(): mean_sq = lax.psum(jnp.sum(matrix * matrix), ('pair', 'rows')) / ncols_all  41.7 us
    dot_general x3, matrix products, local(): turned = jnp.dot(current, rotation, precision=lax.Precision.HIGHEST)  20 us
    dot_general x3, matrix products, local(): lax.dot_general(current, current, (((0,), (0,)), ((), ())), precision=lax...  17.7 us
    ppermute x6, waiting for transfers between devices, local(): lax.ppermute(gram, 'rows', [(dev, dev ^ hop) for dev in range(4)])  15.8 us
  transfers between devices with their start and end apart: 9, of which 6 were waited for; matrix products, arithmetic and copies ran while one was open for 1% of the time, Pallas kernels for 0%

profile of v1, /device:TPU:0, one launch (start us, length us, event | category | flops | bytes accessed | tf_op | source)
XLA Modules:
  0.0 482.1 jit_solution(10297228630206261997)
XLA Ops:
  0.7 10.7 %fusion.76 = f32[256,256]{0,1:T(8,128)S(1)} fusion(f32[4096,256]{1,0:T(8,128)} %param.5), kind=kOutput, calls=%fused_computation.150 | convolution fusion | flops 3221225472 | bytes 4456448 | tf_op jit(solution)/shard_map/dot_general | solution.py:44
  16.9 41.7 %psum.28 = f32[]{:T(128)} all-reduce(f32[]{:T(128)} %multiply_reduce_fusion), channel_id=1, replica_groups=mesh['pair'=8,'rows'=4] {'pair','rows'}, use_global_device_ids=true, to_apply=%region_1.0 | all-reduce | flops 1 | bytes 8 | tf_op jit(solution)/shard_map/psum | solution.py:40
  64.9 11.7 %cholesky.172 = f32[128,128]{1,0:T(8,128)S(1)} custom-call(f32[128,128]{1,0:T(8,128)S(1)} %cholesky.270), custom_call_target="Cholesky" | custom-call | tf_op jit(solution)/shard_map/jit(cholesky)/cholesky | solution.py:29
  76.6 9.8 %custom-call.23 = f32[1,128,128]{1,2,0:T(8,128)S(1)} custom-call(f32[1,128,128]{2,1,0:T(8,128)S(1)} %get-tuple-element.87), custom_call_target="InvertDiagBlocksLowerTriangular" | custom-call | tf_op jit(solution)/shard_map/jit(cholesky)/cholesky | solution.py:29
  86.9 11.7 %cholesky.189 = f32[128,128]{1,0:T(8,128)S(1)} custom-call(f32[128,128]{1,0:T(8,128)S(1)} %convolution_subtract_fusion.11), custom_call_target="Cholesky" | custom-call | tf_op jit(solution)/shard_map/jit(cholesky)/cholesky | solution.py:29
  104.6 19.8 %custom-call.24 = f32[2,128,128]{1,2,0:T(8,128)S(1)} custom-call(f32[2,128,128]{2,1,0:T(8,128)S(1)} %get-tuple-element.24), custom_call_target="InvertDiagBlocksLowerTriangular" | custom-call | tf_op jit(solution)/shard_map/jit(_cho_solve)/triangular_solve | solution.py:30
  126.3 8.8 %convolution_bitcast_fusion = f32[4096,256]{0,1:T(8,128)S(1)} fusion(f32[4096,256]{1,0:T(8,128)} %param.5, f32[128,256]{1,0:T(8,128)S(1)} %fusion.47, f32[128,256]{1,0:T(8,128)S(1)} %fusion.46), kind=kOutput, calls=%fused_computation.9 | convolution fusion | flops 3221291008 | bytes 8650752 | tf_op jit(solution)/shard_map/dot_general | solution.py:63
  137.7 47.2 %collective-permute-done.2 = f32[4096,128]{0,1:T(8,128)S(1)} collective-permute-done((f32[4096,128]{0,1:T(8,128)S(1)}, f32[4096,128]{0,1:T(8,128)S(1)}, u32[]{:S(2)}, u32[]{:S(2)}) %collective-permute-start.2) | collective-permute-done | bytes 2097184 | tf_op jit(solution)/shard_map/ppermute | solution.py:11
  193.5 6.3 %collective-permute-done.4 = f32[256,256]{0,1:T(8,128)S(1)} collective-permute-done((f32[256,256]{0,1:T(8,128)S(1)}, f32[256,256]{0,1:T(8,128)S(1)}, u32[]{:S(2)}, u32[]{:S(2)}) %collective-permute-start.4) | collective-permute-done | bytes 262176 | tf_op jit(solution)/shard_map/ppermute | solution.py:53
  204.7 11.7 %cholesky.206 = f32[128,128]{1,0:T(8,128)S(1)} custom-call(f32[128,128]{1,0:T(8,128)S(1)} %cholesky.273), custom_call_target="Cholesky" | custom-call | tf_op jit(solution)/shard_map/jit(cholesky)/cholesky | solution.py:29
  216.4 9.8 %custom-call.25 = f32[1,128,128]{1,2,0:T(8,128)S(1)} custom-call(f32[1,128,128]{2,1,0:T(8,128)S(1)} %get-tuple-element.83), custom_call_target="InvertDiagBlocksLowerTriangular" | custom-call | tf_op jit(solution)/shard_map/jit(cholesky)/cholesky | solution.py:29
  226.7 11.7 %cholesky.223 = f32[128,128]{1,0:T(8,128)S(1)} custom-call(f32[128,128]{1,0:T(8,128)S(1)} %convolution_subtract_fusion.10), custom_call_target="Cholesky" | custom-call | tf_op jit(solution)/shard_map/jit(cholesky)/cholesky | solution.py:29
  241.0 4.2 while.7
  245.2 19.7 %custom-call.26 = f32[2,128,128]{1,2,0:T(8,128)S(1)} custom-call(f32[2,128,128]{2,1,0:T(8,128)S(1)} %get-tuple-element.25), custom_call_target="InvertDiagBlocksLowerTriangular" | custom-call | tf_op jit(solution)/shard_map/jit(_cho_solve)/triangular_solve | solution.py:30
  266.6 5.6 %fusion.2 = f32[4096,256]{0,1:T(8,128)S(1)} fusion(f32[4096,128]{0,1:T(8,128)} %copy-done.2, f32[4096,128]{0,1:T(8,128)S(1)} %get-tuple-element.74, f32[128,256]{1,0:T(8,128)S(1)} %fusion.50, f32[128,256]{1,0:T(8,128)S(1)} %fusion.49), kind=kOutput, calls=%fused_computation.16 | convolution fusion | flops 3222339584 | bytes 8650752 | tf_op jit(solution)/shard_map/dot_general | solution.py:63
  272.7 49.5 %collective-permute-done.5 = f32[4096,128]{0,1:T(8,128)S(1)} collective-permute-done((f32[4096,128]{0,1:T(8,128)S(1)}, f32[4096,128]{0,1:T(8,128)S(1)}, u32[]{:S(2)}, u32[]{:S(2)}) %collective-permute-start.5) | collective-permute-done | bytes 2097184 | tf_op jit(solution)/shard_map/ppermute | solution.py:11
  329.4 6.4 %collective-permute-done.7 = f32[256,256]{0,1:T(8,128)S(1)} collective-permute-done((f32[256,256]{0,1:T(8,128)S(1)}, f32[256,256]{0,1:T(8,128)S(1)}, u32[]{:S(2)}, u32[]{:S(2)}) %collective-permute-start.7) | collective-permute-done | bytes 262176 | tf_op jit(solution)/shard_map/ppermute | solution.py:53
  340.5 11.7 %cholesky.240 = f32[128,128]{1,0:T(8,128)S(1)} custom-call(f32[128,128]{1,0:T(8,128)S(1)} %cholesky.276), custom_call_target="Cholesky" | custom-call | tf_op jit(solution)/shard_map/jit(cholesky)/cholesky | solution.py:29
  352.3 9.8 %custom-call.27 = f32[1,128,128]{1,2,0:T(8,128)S(1)} custom-call(f32[1,128,128]{2,1,0:T(8,128)S(1)} %get-tuple-element.79), custom_call_target="InvertDiagBlocksLowerTriangular" | custom-call | tf_op jit(solution)/shard_map/jit(cholesky)/cholesky | solution.py:29
  362.6 11.7 %cholesky.257 = f32[128,128]{1,0:T(8,128)S(1)} custom-call(f32[128,128]{1,0:T(8,128)S(1)} %convolution_subtract_fusion.9), custom_call_target="Cholesky" | custom-call | tf_op jit(solution)/shard_map/jit(cholesky)/cholesky | solution.py:29
  381.1 19.7 %custom-call.28 = f32[2,128,128]{1,2,0:T(8,128)S(1)} custom-call(f32[2,128,128]{2,1,0:T(8,128)S(1)} %get-tuple-element.26), custom_call_target="InvertDiagBlocksLowerTriangular" | custom-call | tf_op jit(solution)/shard_map/jit(_cho_solve)/triangular_solve | solution.py:30
  402.5 5.6 %fusion = f32[4096,256]{0,1:T(8,128)S(1)} fusion(f32[4096,128]{0,1:T(8,128)} %copy-done.1, f32[4096,128]{0,1:T(8,128)S(1)} %get-tuple-element.72, f32[128,256]{1,0:T(8,128)S(1)} %fusion.53, f32[128,256]{1,0:T(8,128)S(1)} %fusion.52), kind=kOutput, calls=%fused_computation.14 | convolution fusion | flops 3222339584 | bytes 8650752 | tf_op jit(solution)/shard_map/dot_general | solution.py:63
  409.9 59.8 %all-reduce.1 = (f32[]{:T(128)}, f32[]{:T(128)}, f32[]{:T(128)}) all-reduce(f32[]{:T(128)} %get-tuple-element.62, f32[]{:T(128)} %get-tuple-element.60, f32[]{:T(128)} %get-tuple-element.58), channel_id=1, replica_groups=mesh['pair'=8,'rows'=4] {'pair'}, use_global_device_ids=true, to_apply=%region_11.14 | all-reduce | flops 3 | bytes 24 | tf_op jit(solution)/shard_map/psum | solution.py:15
  476.3 5.6 %copy.29 = f32[4096,256]{1,0:T(8,128)} copy(f32[4096,256]{0,1:T(8,128)} %pad_maximum_fusion.2) | data formatting | bytes 8388608
  (123 shorter events, 73.5 us)
Async XLA Ops:
  0.6 11.9 %copy-start = (f32[4096,256]{1,0:T(8,128)S(1)}, f32[4096,256]{1,0:T(8,128)}, u32[]{:S(2)}) copy-start(f32[4096,256]{1,0:T(8,128)} %param.5) | copy-start | bytes 12582916
  0.6 11.3 %copy-start.3 = (s32[3,1]{0,1:T(1,128)S(1)}, s32[3,1]{0,1:T(1,128)}, u32[]{:S(2)}) copy-start(s32[3,1]{0,1:T(1,128)} %param.6) | copy-start | bytes 40
  11.3 2.9 collective-permute-start
  14.3 45.5 %collective-permute-start.1 = (f32[256,256]{0,1:T(8,128)S(1)}, f32[256,256]{0,1:T(8,128)S(1)}, u32[]{:S(2)}, u32[]{:S(2)}) collective-permute-start(f32[256,256]{0,1:T(8,128)S(1)} %add.116), channel_id=1, source_target_pairs={{0,2},{1,3},{2,0},{3,1},{4,6},{5,7},{6,4},{7,5},{8,10},{9,11},{10,... | collective-permute-start | bytes 786440 | tf_op jit(solution)/shard_map/ppermute | solution.py:53
  135.4 49.5 %collective-permute-start.2 = (f32[4096,128]{0,1:T(8,128)S(1)}, f32[4096,128]{0,1:T(8,128)S(1)}, u32[]{:S(2)}, u32[]{:S(2)}) collective-permute-start(f32[4096,128]{0,1:T(8,128)S(1)} %get-tuple-element.75), channel_id=1, source_target_pairs={{0,4},{4,8},{8,12},{12,16},{16,20},{20,24},{24,28},{28,0},{1,5},{5... | collective-permute-start | bytes 6291464 | tf_op jit(solution)/shard_map/ppermute | solution.py:11
  184.9 1.3 copy-start.2
  189.8 1.6 collective-permute-start.3
  191.4 8.4 %collective-permute-start.4 = (f32[256,256]{0,1:T(8,128)S(1)}, f32[256,256]{0,1:T(8,128)S(1)}, u32[]{:S(2)}, u32[]{:S(2)}) collective-permute-start(f32[256,256]{0,1:T(8,128)S(1)} %add.124), channel_id=1, source_target_pairs={{0,2},{1,3},{2,0},{3,1},{4,6},{5,7},{6,4},{7,5},{8,10},{9,11},{10,... | collective-permute-start | bytes 786440 | tf_op jit(solution)/shard_map/ppermute | solution.py:53
  272.6 49.6 %collective-permute-start.5 = (f32[4096,128]{0,1:T(8,128)S(1)}, f32[4096,128]{0,1:T(8,128)S(1)}, u32[]{:S(2)}, u32[]{:S(2)}) collective-permute-start(f32[4096,128]{0,1:T(8,128)S(1)} %get-tuple-element.73), channel_id=1, source_target_pairs={{0,4},{4,8},{8,12},{12,16},{16,20},{20,24},{24,28},{28,0},{1,5},{5... | collective-permute-start | bytes 6291464 | tf_op jit(solution)/shard_map/ppermute | solution.py:11
  322.2 7.2 %copy-start.1 = (f32[4096,128]{0,1:T(8,128)}, f32[4096,128]{0,1:T(8,128)S(1)}, u32[]{:S(2)}) copy-start(f32[4096,128]{0,1:T(8,128)S(1)} %collective-permute-done.5) | copy-start | bytes 6291460
  325.7 1.6 collective-permute-start.6
  327.4 8.4 %collective-permute-start.7 = (f32[256,256]{0,1:T(8,128)S(1)}, f32[256,256]{0,1:T(8,128)S(1)}, u32[]{:S(2)}, u32[]{:S(2)}) collective-permute-start(f32[256,256]{0,1:T(8,128)S(1)} %add.131), channel_id=1, source_target_pairs={{0,2},{1,3},{2,0},{3,1},{4,6},{5,7},{6,4},{7,5},{8,10},{9,11},{10,... | collective-permute-start | bytes 786440 | tf_op jit(solution)/shard_map/ppermute | solution.py:53
  409.9 62.5 %collective-permute-start.8 = (f32[4096,128]{0,1:T(8,128)}, f32[4096,128]{0,1:T(8,128)}, u32[]{:S(2)}, u32[]{:S(2)}) collective-permute-start(f32[4096,128]{0,1:T(8,128)} %get-tuple-element.71), channel_id=1, source_target_pairs={{0,4},{4,8},{8,12},{12,16},{16,20},{20,24},{24,28},{28,0},{1,5},{5... | collective-permute-start | bytes 6291464 | tf_op jit(solution)/shard_map/ppermute | solution.py:11
